TPU v7x, 32 devices: a whole 2x2x4 slice. The times are simulated.
32 devices in a mesh: rows: 8 (over z, y), cols: 4 (over x, core).
Axes of the slice: x: 2, y: 2, z: 4, core: 2. Of those that a mesh axis runs over, the one named last changes fastest.
Arguments:
- right_leaf: float32 [4, 2048, 128], P(None, 'rows'), may hold values from -6 to 6
- right_mid: float32 [2, 4096, 128], P(None, 'rows'), may hold values from -6 to 6
- right_root: float32 [8192, 128], P('rows'), may hold values from -6 to 6
- inverse_leaf: float32 [4, 2048, 2048], P(None, 'rows', 'cols'), may hold values from -1 to 2, as said below
- inverse_mid: float32 [2, 4096, 4096], P(None, 'rows', 'cols'), may hold values from -1 to 2, as said below
- inverse_root: float32 [8192, 8192], P('rows', 'cols'), may hold values from -1 to 2, as said below
- leaf_to_mid: float32 [4, 4096, 2048], P(None, 'rows', 'cols'), may hold values from -0.125 to 0.125
- leaf_to_root: float32 [4, 8192, 2048], P(None, 'rows', 'cols'), may hold values from -0.125 to 0.125
- mid_to_root: float32 [2, 8192, 4096], P(None, 'rows', 'cols'), may hold values from -0.09375 to 0.09375
- mask_leaf_mid: int32 [4, 32, 16], replicated, may hold values 0 or 1
- mask_leaf_root: int32 [4, 64, 16], replicated, may hold values 0 or 1
- mask_mid_root: int32 [2, 64, 32], replicated, may hold values 0 or 1
Outputs:
- solved_leaf: float32 [4, 2048, 128], P(None, 'rows')
- solved_mid: float32 [2, 4096, 128], P(None, 'rows')
- solved_root: float32 [8192, 128], P('rows')
Inputs may be any that keep to these rules, and one draw needn't show every extreme that they name: `inverse_leaf`: lower triangular, with its diagonal between 0.5 and 2. `inverse_mid`: lower triangular, with its diagonal between 0.5 and 2. `inverse_root`: lower triangular, with its diagonal between 0.5 and 2.
All inputs are finite; a program needn't handle non-finite values.
Results may differ from a plain program's by a relative error of at most 0.00014.
Values sent between devices are 32-bit elements; how exact they have to be, the bound alone decides.
No kernel may reach another device: no remote copies, remote signals or barrier semaphores. Data moves between devices by JAX's collectives and lax.ppermute only.
A program may use at most 128 MiB of HBM per device.

v0:
```python
import jax
import jax.numpy as jnp
from jax import lax
from jax.sharding import PartitionSpec as P

TILE = 128


def product(matrix, vector):
    return jnp.einsum(
        "src,sck->srk",
        matrix,
        vector,
        precision=lax.Precision.HIGHEST,
        preferred_element_type=jnp.float32,
    )


def own_columns(gathered):
    col_width = gathered.shape[1] // lax.axis_size("cols")
    return lax.dynamic_slice_in_dim(gathered, lax.axis_index("cols") * col_width, col_width, 1)


def masked(values, pattern):
    rows_dev = values.shape[1]
    cols_dev = values.shape[2]
    row_ids = lax.axis_index("rows") * rows_dev + lax.iota(jnp.int32, rows_dev)
    col_ids = lax.axis_index("cols") * cols_dev + lax.iota(jnp.int32, cols_dev)
    row_hot = (row_ids[:, None] // TILE == lax.iota(jnp.int32, pattern.shape[1])[None, :]).astype(
        jnp.float32
    )
    col_hot = (col_ids[:, None] // TILE == lax.iota(jnp.int32, pattern.shape[2])[None, :]).astype(
        jnp.float32
    )
    expanded = jnp.einsum("ra,sab,cb->src", row_hot, pattern.astype(jnp.float32), col_hot)
    return values * expanded


def fetch_columns(block):
    gathered = lax.all_gather(block, "rows", axis=1, tiled=True)
    return own_columns(gathered)


def solve_block(residual, inverse, spread_needed):
    partial_value = product(inverse, fetch_columns(residual))
    solved = lax.psum(partial_value, "cols")
    spread = fetch_columns(solved) if spread_needed else solved
    return (solved, spread)


def body(
    right_leaf,
    right_mid,
    right_root,
    inverse_leaf,
    inverse_mid,
    inverse_root,
    leaf_to_mid,
    leaf_to_root,
    mid_to_root,
    mask_leaf_mid,
    mask_leaf_root,
    mask_mid_root,
):
    factor_lm = masked(leaf_to_mid, mask_leaf_mid)
    factor_lr = masked(leaf_to_root, mask_leaf_root)
    factor_mr = masked(mid_to_root, mask_mid_root)
    solved_leaf, leaf_columns = solve_block(right_leaf, inverse_leaf, True)
    mid_terms = product(factor_lm, leaf_columns)
    mid_part = mid_terms.reshape(2, 2, mid_terms.shape[1], mid_terms.shape[2]).sum(axis=1)
    root_part = product(factor_lr, leaf_columns).sum(axis=0)[None]
    mid_summed, root_summed = lax.psum((mid_part, root_part), "cols")
    resid_mid = right_mid - mid_summed
    solved_mid, mid_columns = solve_block(resid_mid, inverse_mid, True)
    root_more = product(factor_mr, mid_columns).sum(axis=0)[None]
    resid_root = right_root[None] - root_summed - lax.psum(root_more, "cols")
    solved_root, unused_spread = solve_block(resid_root, inverse_root[None], False)
    return (solved_leaf, solved_mid, solved_root[0])


def solution(mesh):
    placed = (
        P(None, "rows", None),
        P(None, "rows", None),
        P("rows", None),
        P(None, "rows", "cols"),
        P(None, "rows", "cols"),
        P("rows", "cols"),
        P(None, "rows", "cols"),
        P(None, "rows", "cols"),
        P(None, "rows", "cols"),
        P(),
        P(),
        P(),
    )
    return jax.shard_map(
        body,
        mesh=mesh,
        in_specs=placed,
        out_specs=(P(None, "rows", None), P(None, "rows", None), P("rows", None)),
        check_vma=False,
    )
```

profile of v0, /device:TPU:0, one launch (start us, length us, event | category | flops | bytes accessed | tf_op | source)
XLA Modules:
  0.0 608.7 jit_solution(15092546820964897420)
XLA Ops:
  7.2 0.0 copy-start
  7.2 0.0 copy-start.6
  7.2 0.0 all-gather.6.cloned.1.call-start
  7.2 2.2 copy.32
  9.4 0.0 all-gather.6.cloned.1.call-update
  9.4 0.0 all-reduce.7.cloned.1.call-start
  9.5 78.9 %all-gather.6.cloned.1.call-done = f32[4,2048,128]{1,2,0:T(8,128)} async-done(((f32[4,256,128]{1,2,0:T(8,128)}), f32[4,2048,128]{1,2,0:T(8,128)}) %all-gather.6.cloned.1.call-update) | async-done | bytes 4194320 | tf_op jit(solution)/shard_map/all_gather | solution.py:40
  88.4 0.0 copy-done
  88.4 4.2 convolution_bitcast_fusion.1
  92.6 0.0 all-reduce.7.cloned.1.call-update
  92.6 0.0 all-gather.8.cloned.1.call-start
  92.7 31.4 %all-reduce.7.cloned.1.call-done = f32[4,256,128]{1,2,0:T(8,128)} async-done(((f32[4,256,128]{1,2,0:T(8,128)}), f32[4,256,128]{1,2,0:T(8,128)}) %all-reduce.7.cloned.1.call-update) | async-done | bytes 524304 | tf_op jit(solution)/shard_map/psum | solution.py:46
  124.1 0.0 all-gather.8.cloned.1.call-update
  124.1 0.0 all-reduce.9.cloned.1.call-start
  124.2 0.0 copy-done.6
  124.3 0.2 fusion.32
  124.4 2.7 fusion.37
  127.1 74.1 %all-gather.8.cloned.1.call-done = f32[4,2048,128]{1,2,0:T(8,128)} async-done(((f32[4,256,128]{1,2,0:T(8,128)}), f32[4,2048,128]{1,2,0:T(8,128)}) %all-gather.8.cloned.1.call-update) | async-done | bytes 4194320 | tf_op jit(solution)/shard_map/all_gather | solution.py:40
  201.2 7.5 %bitcast_reduce_fusion = f32[2,512,128]{2,1,0:T(8,128)S(1)} fusion(f32[4,2048,128]{1,2,0:T(8,128)} %all-gather.8.cloned.1.call-done, s32[]{:T(128)S(6)} %select_n.49, f32[4,512,512]{2,1,0:T(8,128)} %param.18, f32[4,512,512]{2,1,0:T(8,128)} %fusion.37), kind=kOutput, calls=%fused_computation.12 | convolution fusion | flops 1611792384 | bytes 9961476 | tf_op jit(solution)/shard_map/src,sck->srk/dot_general | solution.py:10
  208.7 1.0 copy.34
  209.7 0.0 all-reduce.9.cloned.1.call-update
  209.7 0.0 all-gather.10.cloned.1.call-start
  209.8 0.0 copy-done.4
  209.8 0.2 copy.35
  210.0 0.0 copy-start.7
  210.0 0.0 copy-start.8
  210.0 31.2 %all-reduce.9.cloned.1.call-done = f32[2,512,128]{1,2,0:T(8,128)} async-done(((f32[2,512,128]{1,2,0:T(8,128)}), f32[2,512,128]{1,2,0:T(8,128)}) %all-reduce.9.cloned.1.call-update) | async-done | bytes 524304 | tf_op jit(solution)/shard_map/psum | solution.py:72
  241.3 1.9 sub.35
  243.2 0.0 all-gather.10.cloned.1.call-update
  243.2 0.0 all-reduce.11.cloned.1.call-start
  243.3 74.0 %all-gather.10.cloned.1.call-done = f32[2,4096,128]{1,2,0:T(8,128)} async-done(((f32[2,512,128]{1,2,0:T(8,128)}), f32[2,4096,128]{1,2,0:T(8,128)}) %all-gather.10.cloned.1.call-update) | async-done | bytes 4194320 | tf_op jit(solution)/shard_map/all_gather | solution.py:40
  317.3 7.7 %convolution_bitcast_fusion.2 = f32[2,512,128]{1,2,0:T(8,128)} fusion(f32[2,512,1024]{2,1,0:T(8,128)} %param.16, f32[2,4096,128]{1,2,0:T(8,128)} %all-gather.10.cloned.1.call-done, s32[]{:T(128)S(6)} %select_n.52), kind=kOutput, calls=%fused_computation.10 | convolution fusion | flops 1610612736 | bytes 5767172 | tf_op jit(solution)/shard_map/src,sck->srk/dot_general | solution.py:10
  325.0 0.0 all-reduce.11.cloned.1.call-update
  325.0 0.0 all-gather.12.cloned.1.call-start
  325.0 31.5 %all-reduce.11.cloned.1.call-done = f32[2,512,128]{1,2,0:T(8,128)} async-done(((f32[2,512,128]{1,2,0:T(8,128)}), f32[2,512,128]{1,2,0:T(8,128)}) %all-reduce.11.cloned.1.call-update) | async-done | bytes 524304 | tf_op jit(solution)/shard_map/psum | solution.py:46
  356.6 0.0 all-gather.12.cloned.1.call-update
  356.6 0.2 all-reduce.15.cloned.1.call-start
  356.8 0.0 copy-done.7
  356.9 0.0 copy-done.8
  356.9 0.2 fusion.24
  357.1 0.2 fusion.25
  357.3 0.0 slice-start
  357.3 1.3 fusion.35
  358.6 0.0 slice-start.1
  358.6 4.5 fusion.29
  363.1 0.0 slice-done
  363.1 8.7 %fusion.6 = f32[1,1024,128]{2,1,0:T(8,128)} fusion(f32[4,1024,512]{2,1,0:T(8,128)S(1)} %bitcast.56, f32[4,1024,512]{2,1,0:T(8,128)S(1)} %fusion.35, f32[4,2048,128]{1,2,0:T(8,128)} %all-gather.8.cloned.1.call-done, s32[]{:T(128)S(6)} %select_n.49), kind=kOutput, calls=%fused_computation.6 | convolution fusion | flops 3223322624 | bytes 18350084 | tf_op jit(solution)/shard_map/src,sck->srk/dot_general | solution.py:10
  371.9 60.3 %all-gather.12.cloned.1.call-done = f32[2,4096,128]{1,2,0:T(8,128)} async-done(((f32[2,512,128]{1,2,0:T(8,128)}), f32[2,4096,128]{1,2,0:T(8,128)}) %all-gather.12.cloned.1.call-update) | async-done | bytes 4194320 | tf_op jit(solution)/shard_map/all_gather | solution.py:40
  432.2 11.2 %fusion.9 = f32[1,1024,128]{2,1,0:T(8,128)} fusion(f32[2,1024,1024]{2,1,0:T(8,128)} %param.20, f32[2,1024,1024]{2,1,0:T(8,128)} %fusion.29, f32[2,4096,128]{1,2,0:T(8,128)} %all-gather.12.cloned.1.call-done, s32[]{:T(128)S(6)} %select_n.52), kind=kOutput, calls=%fused_computation.7 | convolution fusion | flops 3223322624 | bytes 18350084 | tf_op jit(solution)/shard_map/src,sck->srk/dot_general | solution.py:10
  443.4 0.0 all-reduce.15.cloned.1.call-update
  443.5 0.0 all-gather.14.cloned.1.call-start
  443.5 34.5 %all-reduce.15.cloned.1.call-done = (f32[1,1024,128]{2,1,0:T(8,128)}, f32[1,1024,128]{2,1,0:T(8,128)}) async-done(((f32[1,1024,128]{2,1,0:T(8,128)}, f32[1,1024,128]{2,1,0:T(8,128)}), (f32[1,1024,128]{2,1,0:T(8,128)}, f32[1,1024,128]{2,1,0:T(8,128)})) %all-reduce.15.cloned.1.call-update) | async-done | bytes 1048592 | tf_op jit(solution)/shard_map/psum | solution.py:76
  478.1 0.0 copy-done.5
  478.1 2.1 fusion.23
  480.1 0.0 all-gather.14.cloned.1.call-update
  480.2 0.0 all-reduce.13.cloned.1.call-start
  480.2 74.6 %all-gather.14.cloned.1.call-done = f32[1,8192,128]{2,1,0:T(8,128)} async-done(((f32[1,1024,128]{2,1,0:T(8,128)}), f32[1,8192,128]{2,1,0:T(8,128)}) %all-gather.14.cloned.1.call-update) | async-done | bytes 4194320 | tf_op jit(solution)/shard_map/all_gather | solution.py:40
  554.8 13.4 %convolution_bitcast_fusion = f32[1024,128]{0,1:T(8,128)} fusion(f32[1024,2048]{1,0:T(8,128)} %param.17, f32[1,8192,128]{2,1,0:T(8,128)} %all-gather.14.cloned.1.call-done, s32[]{:T(128)S(6)} %select_n.55), kind=kOutput, calls=%fused_computation.8 | convolution fusion | flops 3221225472 | bytes 9961476 | tf_op jit(solution)/shard_map/src,sck->srk/dot_general | solution.py:10
  568.3 0.0 all-reduce.13.cloned.1.call-update
  568.3 1.0 copy.38
  569.3 1.0 copy.39
  570.3 29.6 %all-reduce.13.cloned.1.call-done = f32[1024,128]{0,1:T(8,128)} async-done(((f32[1024,128]{0,1:T(8,128)}), f32[1024,128]{0,1:T(8,128)}) %all-reduce.13.cloned.1.call-update) | async-done | bytes 524304 | tf_op jit(solution)/shard_map/psum | solution.py:46
  599.9 2.0 copy.40
  601.9 0.0 copy-done.1
  (16 shorter events, 0.1 us)
Async XLA Ops:
  7.2 81.2 %copy-start = (f32[4,256,512]{2,1,0:T(8,128)S(1)}, f32[4,256,512]{2,1,0:T(8,128)}, u32[]{:S(2)}) copy-start(f32[4,256,512]{2,1,0:T(8,128)} %param.15) | copy-start | bytes 6291460
  7.2 117.0 %copy-start.6 = (s32[4,32,16]{1,2,0:T(8,128)S(1)}, s32[4,32,16]{1,2,0:T(8,128)}, u32[]{:S(2)}) copy-start(s32[4,32,16]{1,2,0:T(8,128)} %param.21) | copy-start | bytes 24580
  7.2 81.2 %all-gather.6.cloned.1.call-start = ((), (), s32[]{:S(2)}) async-start(), calls=%async_computation | async-start | bytes 4718592 | tf_op jit(solution)/shard_map/all_gather | solution.py:40
  9.4 114.7 %all-reduce.7.cloned.1.call-start = ((), (), s32[]{:S(2)}) async-start(), calls=%async_computation.1 | async-start | bytes 1048576 | tf_op jit(solution)/shard_map/psum | solution.py:46
  92.6 108.6 %all-gather.8.cloned.1.call-start = ((), (), s32[]{:S(2)}) async-start(), calls=%async_computation.2 | async-start | bytes 4718592 | tf_op jit(solution)/shard_map/all_gather | solution.py:40
  124.1 117.1 %all-reduce.9.cloned.1.call-start = ((), (), s32[]{:S(2)}) async-start(), calls=%async_computation.3 | async-start | bytes 1048576 | tf_op jit(solution)/shard_map/psum | solution.py:72
  127.1 82.7 %copy-start.4 = (f32[2,512,128]{2,1,0:T(8,128)S(1)}, f32[2,512,128]{2,1,0:T(8,128)}, u32[]{:S(2)}) copy-start(f32[2,512,128]{2,1,0:T(8,128)} %param.13) | copy-start | bytes 1572868
  209.7 107.5 %all-gather.10.cloned.1.call-start = ((), (), s32[]{:S(2)}) async-start(), calls=%async_computation.4 | async-start | bytes 4718592 | tf_op jit(solution)/shard_map/all_gather | solution.py:40
  210.0 146.8 %copy-start.7 = (s32[2,64,32]{1,2,0:T(8,128)S(1)}, s32[2,64,32]{1,2,0:T(8,128)}, u32[]{:S(2)}) copy-start(s32[2,64,32]{1,2,0:T(8,128)} %param.23) | copy-start | bytes 49156
  210.0 146.8 %copy-start.8 = (s32[4,64,16]{1,2,0:T(8,128)S(1)}, s32[4,64,16]{1,2,0:T(8,128)}, u32[]{:S(2)}) copy-start(s32[4,64,16]{1,2,0:T(8,128)} %param.22) | copy-start | bytes 49156
  243.2 113.4 %all-reduce.11.cloned.1.call-start = ((), (), s32[]{:S(2)}) async-start(), calls=%async_computation.5 | async-start | bytes 1048576 | tf_op jit(solution)/shard_map/psum | solution.py:46
  325.0 107.2 %all-gather.12.cloned.1.call-start = ((), (), s32[]{:S(2)}) async-start(), calls=%async_computation.6 | async-start | bytes 4718592 | tf_op jit(solution)/shard_map/all_gather | solution.py:40
  356.6 121.5 %all-reduce.15.cloned.1.call-start = ((), (), s32[]{:S(2)}) async-start(), calls=%async_computation.9 | async-start | bytes 2097152 | tf_op jit(solution)/shard_map/psum | solution.py:76
  357.3 5.8 slice-start
  358.6 4.6 slice-start.1
  371.9 106.2 %copy-start.5 = (f32[1024,128]{1,0:T(8,128)S(1)}, f32[1024,128]{1,0:T(8,128)}, u32[]{:S(2)}) copy-start(f32[1024,128]{1,0:T(8,128)} %param.14) | copy-start | bytes 1572868
  443.5 111.4 %all-gather.14.cloned.1.call-start = ((), (), s32[]{:S(2)}) async-start(), calls=%async_computation.7 | async-start | bytes 4718592 | tf_op jit(solution)/shard_map/all_gather | solution.py:40
  480.2 119.7 %all-reduce.13.cloned.1.call-start = ((), (), s32[]{:S(2)}) async-start(), calls=%async_computation.8 | async-start | bytes 1048576 | tf_op jit(solution)/shard_map/psum | solution.py:46
  480.2 88.1 %copy-start.2 = (f32[4,256,128]{1,2,0:T(8,128)S(1)}, f32[4,256,128]{1,2,0:T(8,128)}, u32[]{:S(2)}) copy-start(f32[4,256,128]{1,2,0:T(8,128)} %all-reduce.7.cloned.1.call-done) | copy-start | bytes 1572868
  480.2 89.1 %copy-start.3 = (f32[2,512,128]{1,2,0:T(8,128)S(1)}, f32[2,512,128]{1,2,0:T(8,128)}, u32[]{:S(2)}) copy-start(f32[2,512,128]{1,2,0:T(8,128)} %all-reduce.11.cloned.1.call-done) | copy-start | bytes 1572868
  554.8 47.1 %copy-start.1 = (f32[4,256,512]{2,1,0:T(8,128)S(1)}, f32[4,256,512]{2,1,0:T(8,128)}, u32[]{:S(2)}) copy-start(f32[4,256,512]{2,1,0:T(8,128)} %param.15) | copy-start | bytes 6291460
Sparse Core Ops, SparseCore 0:
  10.6 77.7 all-gather.5
  92.8 31.3 all-reduce.6
  126.2 75.0 all-gather.7
  209.9 31.3 all-reduce.8
  243.9 73.3 all-gather.9
  325.1 31.4 all-reduce.10
  358.8 73.3 all-gather.11
  443.6 34.4 all-reduce.14
  481.0 73.8 all-gather.13
  568.4 31.4 all-reduce.12
where the time goes:
time: 609 us
  waiting for transfers between devices  520 us (85%)
  matrix products  61.8 us (10%)
  between operations  14.4 us (2%)
  local copies, waits for them, and re-layouts  7.45 us (1%)
    all_gather x5, waiting for transfers between devices, fetch_columns(): gathered = lax.all_gather(block, 'rows', axis=1, tiled=True)  362 us
    psum x3, waiting for transfers between devices, solve_block(): solved = lax.psum(partial_value, 'cols')  92.6 us
    dot_general x6, matrix products, product(): jnp.einsum('src,sck->srk', matrix, vector, precision=lax.Precision.HIGHES...  52.8 us
    psum x1, waiting for transfers between devices, body(): resid_root = right_root[None] - root_summed - lax.psum(root_more, 'cols')  34.5 us
    psum x1, waiting for transfers between devices, body(): mid_summed, root_summed = lax.psum((mid_part, root_part), 'cols')  31.2 us
  transfers between devices with their start and end apart: 10, of which 10 were waited for; matrix products, arithmetic and copies ran while one was open for 3% of the time, Pallas kernels for 0%

commit v1 on v0

--- a/solution.py
+++ b/solution.py
@@ -43,7 +43,9 @@
 
 def solve_block(residual, inverse, spread_needed):
     partial_value = product(inverse, fetch_columns(residual))
-    solved = lax.psum(partial_value, "cols")
+    solved = partial_value
+    for hop in (1, 2):
+        solved = solved + lax.ppermute(solved, "cols", [(dev, dev ^ hop) for dev in range(4)])
     spread = fetch_columns(solved) if spread_needed else solved
     return (solved, spread)
 

time: 609 us -> 553 us (0.908)
  waiting for transfers between devices: 520 us -> 462 us
    psum x3 -> x0, waiting for transfers between devices: 92.6 us -> none  [solve_block(): solved = lax.psum(partial_value, 'cols')]
    ppermute x0 -> x6, waiting for transfers between devices: none -> 41.5 us  [solve_block(): lax.ppermute(solved, 'cols', [(dev, dev ^ hop) for dev in range(4)])]
    all_gather x5, waiting for transfers between devices: 362 us -> 354 us  [fetch_columns(): gathered = lax.all_gather(block, 'rows', axis=1, tiled=True)]
  transfers between devices with their start and end apart: 10 -> 13, of which waited for: 10 -> 13; matrix products, arithmetic and copies ran while one was open for 3% -> 4% of each run, Pallas kernels for 0% -> 0%
where the time goes in v1:
time: 553 us
  waiting for transfers between devices  462 us (84%)
  matrix products  56.7 us (10%)
  between operations  14.4 us (3%)
  other arithmetic  8.05 us (1%)
  local copies, waits for them, and re-layouts  6.42 us (1%)
    all_gather x5, waiting for transfers between devices, fetch_columns(): gathered = lax.all_gather(block, 'rows', axis=1, tiled=True)  354 us
    dot_general x6, matrix products, product(): jnp.einsum('src,sck->srk', matrix, vector, precision=lax.Precision.HIGHES...  47.7 us
    ppermute x6, waiting for transfers between devices, solve_block(): lax.ppermute(solved, 'cols', [(dev, dev ^ hop) for dev in range(4)])  41.5 us
    psum x1, waiting for transfers between devices, body(): resid_root = right_root[None] - root_summed - lax.psum(root_more, 'cols')  34.6 us
    psum x1, waiting for transfers between devices, body(): mid_summed, root_summed = lax.psum((mid_part, root_part), 'cols')  31.3 us
  transfers between devices with their start and end apart: 13, of which 13 were waited for; matrix products, arithmetic and copies ran while one was open for 4% of the time, Pallas kernels for 0%

profile of v1, /device:TPU:0, one launch (start us, length us, event | category | flops | bytes accessed | tf_op | source)
XLA Modules:
  0.0 552.6 jit_solution(17881133041655894282)
XLA Ops:
  7.2 0.0 copy-start
  7.2 0.0 all-gather.6.cloned.1.call-start
  7.2 2.2 copy.32
  9.4 0.0 all-gather.6.cloned.1.call-update
  9.4 0.0 all-gather.8.cloned.1.call-start
  9.5 78.9 %all-gather.6.cloned.1.call-done = f32[4,2048,128]{1,2,0:T(8,128)} async-done(((f32[4,256,128]{1,2,0:T(8,128)}), f32[4,2048,128]{1,2,0:T(8,128)}) %all-gather.6.cloned.1.call-update) | async-done | bytes 4194320 | tf_op jit(solution)/shard_map/all_gather | solution.py:40
  88.4 3.4 convolution_bitcast_fusion.1
  91.8 0.1 collective-permute-start
  91.9 1.9 collective-permute-done
  93.8 0.1 add.104
  93.9 1.5 collective-permute-start.1
  95.4 12.5 %collective-permute-done.1 = f32[4,256,128]{1,2,0:T(8,128)S(1)} collective-permute-done((f32[4,256,128]{1,2,0:T(8,128)S(1)}, f32[4,256,128]{1,2,0:T(8,128)S(1)}, u32[]{:S(2)}, u32[]{:S(2)}) %collective-permute-start.1) | collective-permute-done | bytes 524320 | tf_op jit(solution)/shard_map/ppermute | solution.py:48
  107.9 0.9 add.105
  108.8 0.0 all-gather.8.cloned.1.call-update
  108.8 0.0 all-reduce.4.cloned.1.call-start
  108.9 0.1 fusion.32
  109.0 2.7 fusion.37
  111.7 70.4 %all-gather.8.cloned.1.call-done = f32[4,2048,128]{1,2,0:T(8,128)} async-done(((f32[4,256,128]{1,2,0:T(8,128)}), f32[4,2048,128]{1,2,0:T(8,128)}) %all-gather.8.cloned.1.call-update) | async-done | bytes 4194320 | tf_op jit(solution)/shard_map/all_gather | solution.py:40
  182.1 7.5 %bitcast_reduce_fusion = f32[2,512,128]{2,1,0:T(8,128)S(1)} fusion(f32[4,2048,128]{1,2,0:T(8,128)} %all-gather.8.cloned.1.call-done, s32[]{:T(128)S(6)} %select_n.49, f32[4,512,512]{2,1,0:T(8,128)} %param.18, f32[4,512,512]{2,1,0:T(8,128)} %fusion.37), kind=kOutput, calls=%fused_computation.12 | convolution fusion | flops 1611792384 | bytes 9961476 | tf_op jit(solution)/shard_map/src,sck->srk/dot_general | solution.py:10
  189.6 1.0 copy.34
  190.6 0.0 all-reduce.4.cloned.1.call-update
  190.7 0.0 all-gather.10.cloned.1.call-start
  190.7 0.2 copy.35
  190.9 31.3 %all-reduce.4.cloned.1.call-done = f32[2,512,128]{1,2,0:T(8,128)} async-done(((f32[2,512,128]{1,2,0:T(8,128)}), f32[2,512,128]{1,2,0:T(8,128)}) %all-reduce.4.cloned.1.call-update) | async-done | bytes 524304 | tf_op jit(solution)/shard_map/psum | solution.py:74
  222.2 1.9 sub.35
  224.1 0.0 all-gather.10.cloned.1.call-update
  224.1 0.0 all-gather.12.cloned.1.call-start
  224.2 0.0 copy-start.8
  224.2 74.0 %all-gather.10.cloned.1.call-done = f32[2,4096,128]{1,2,0:T(8,128)} async-done(((f32[2,512,128]{1,2,0:T(8,128)}), f32[2,4096,128]{1,2,0:T(8,128)}) %all-gather.10.cloned.1.call-update) | async-done | bytes 4194320 | tf_op jit(solution)/shard_map/all_gather | solution.py:40
  298.2 6.9 %convolution_bitcast_fusion.2 = f32[2,512,128]{1,2,0:T(8,128)S(1)} fusion(f32[2,512,1024]{2,1,0:T(8,128)} %param.16, f32[2,4096,128]{1,2,0:T(8,128)} %all-gather.10.cloned.1.call-done, s32[]{:T(128)S(6)} %select_n.52), kind=kOutput, calls=%fused_computation.10 | convolution fusion | flops 1610612736 | bytes 5767172 | tf_op jit(solution)/shard_map/src,sck->srk/dot_general | solution.py:10
  305.1 0.1 collective-permute-start.2
  305.2 1.9 collective-permute-done.2
  307.1 0.1 add.111
  307.2 1.5 collective-permute-start.3
  308.7 12.5 %collective-permute-done.3 = f32[2,512,128]{1,2,0:T(8,128)S(1)} collective-permute-done((f32[2,512,128]{1,2,0:T(8,128)S(1)}, f32[2,512,128]{1,2,0:T(8,128)S(1)}, u32[]{:S(2)}, u32[]{:S(2)}) %collective-permute-start.3) | collective-permute-done | bytes 524320 | tf_op jit(solution)/shard_map/ppermute | solution.py:48
  321.2 0.9 add.112
  322.1 0.0 all-gather.12.cloned.1.call-update
  322.1 0.2 all-reduce.6.cloned.1.call-start
  322.4 0.2 fusion.24
  322.6 0.2 fusion.25
  322.8 0.0 slice-start
  322.8 1.3 fusion.35
  324.1 0.0 slice-start.1
  324.1 4.6 fusion.29
  328.6 8.8 %fusion.6 = f32[1,1024,128]{2,1,0:T(8,128)} fusion(f32[4,1024,512]{2,1,0:T(8,128)S(1)} %bitcast.60, f32[4,1024,512]{2,1,0:T(8,128)S(1)} %fusion.35, f32[4,2048,128]{1,2,0:T(8,128)} %all-gather.8.cloned.1.call-done, s32[]{:T(128)S(6)} %select_n.49), kind=kOutput, calls=%fused_computation.6 | convolution fusion | flops 3223322624 | bytes 18350084 | tf_op jit(solution)/shard_map/src,sck->srk/dot_general | solution.py:10
  337.4 56.5 %all-gather.12.cloned.1.call-done = f32[2,4096,128]{1,2,0:T(8,128)} async-done(((f32[2,512,128]{1,2,0:T(8,128)}), f32[2,4096,128]{1,2,0:T(8,128)}) %all-gather.12.cloned.1.call-update) | async-done | bytes 4194320 | tf_op jit(solution)/shard_map/all_gather | solution.py:40
  393.9 11.2 %fusion.9 = f32[1,1024,128]{2,1,0:T(8,128)} fusion(f32[2,1024,1024]{2,1,0:T(8,128)} %param.20, f32[2,1024,1024]{2,1,0:T(8,128)} %fusion.29, f32[2,4096,128]{1,2,0:T(8,128)} %all-gather.12.cloned.1.call-done, s32[]{:T(128)S(6)} %select_n.52), kind=kOutput, calls=%fused_computation.7 | convolution fusion | flops 3223322624 | bytes 18350084 | tf_op jit(solution)/shard_map/src,sck->srk/dot_general | solution.py:10
  405.1 0.0 all-reduce.6.cloned.1.call-update
  405.2 0.0 all-gather.14.cloned.1.call-start
  405.2 34.6 %all-reduce.6.cloned.1.call-done = (f32[1,1024,128]{2,1,0:T(8,128)}, f32[1,1024,128]{2,1,0:T(8,128)}) async-done(((f32[1,1024,128]{2,1,0:T(8,128)}, f32[1,1024,128]{2,1,0:T(8,128)}), (f32[1,1024,128]{2,1,0:T(8,128)}, f32[1,1024,128]{2,1,0:T(8,128)})) %all-reduce.6.cloned.1.call-update) | async-done | bytes 1048592 | tf_op jit(solution)/shard_map/psum | solution.py:78
  439.8 2.1 fusion.23
  441.8 0.0 all-gather.14.cloned.1.call-update
  441.9 0.0 copy-start.2
  441.9 74.6 %all-gather.14.cloned.1.call-done = f32[1,8192,128]{2,1,0:T(8,128)} async-done(((f32[1,1024,128]{2,1,0:T(8,128)}), f32[1,8192,128]{2,1,0:T(8,128)}) %all-gather.14.cloned.1.call-update) | async-done | bytes 4194320 | tf_op jit(solution)/shard_map/all_gather | solution.py:40
  516.5 9.9 %convolution_bitcast_fusion = f32[1,1024,128]{1,2,0:T(8,128)S(1)} fusion(f32[1024,2048]{1,0:T(8,128)} %param.17, f32[1,8192,128]{2,1,0:T(8,128)} %all-gather.14.cloned.1.call-done, s32[]{:T(128)S(6)} %select_n.55), kind=kOutput, calls=%fused_computation.8 | convolution fusion | flops 3221225472 | bytes 9961476 | tf_op jit(solution)/shard_map/src,sck->srk/dot_general | solution.py:10
  526.4 0.1 collective-permute-start.4
  526.5 1.9 collective-permute-done.4
  528.4 0.9 add.118
  529.3 1.5 collective-permute-start.5
  530.7 1.0 copy.38
  531.7 1.0 copy.39
  532.7 10.8 %collective-permute-done.5 = f32[1,1024,128]{1,2,0:T(8,128)} collective-permute-done((f32[1,1024,128]{1,2,0:T(8,128)}, f32[1,1024,128]{1,2,0:T(8,128)}, u32[]{:S(2)}, u32[]{:S(2)}) %collective-permute-start.5) | collective-permute-done | bytes 524320 | tf_op jit(solution)/shard_map/ppermute | solution.py:48
  543.5 1.3 add_bitcast_fusion
  544.8 1.0 copy.40
  (25 shorter events, 0.1 us)
Async XLA Ops:
  7.2 81.2 %copy-start = (f32[4,256,512]{2,1,0:T(8,128)S(1)}, f32[4,256,512]{2,1,0:T(8,128)}, u32[]{:S(2)}) copy-start(f32[4,256,512]{2,1,0:T(8,128)} %param.15) | copy-start | bytes 6291460
  7.2 81.2 %all-gather.6.cloned.1.call-start = ((), (), s32[]{:S(2)}) async-start(), calls=%async_computation | async-start | bytes 4718592 | tf_op jit(solution)/shard_map/all_gather | solution.py:40
  9.4 99.4 %copy-start.6 = (s32[4,32,16]{1,2,0:T(8,128)S(1)}, s32[4,32,16]{1,2,0:T(8,128)}, u32[]{:S(2)}) copy-start(s32[4,32,16]{1,2,0:T(8,128)} %param.21) | copy-start | bytes 24580
  9.4 172.7 %all-gather.8.cloned.1.call-start = ((), (), s32[]{:S(2)}) async-start(), calls=%async_computation.1 | async-start | bytes 4718592 | tf_op jit(solution)/shard_map/all_gather | solution.py:40
  91.8 2.0 collective-permute-start
  93.9 14.0 %collective-permute-start.1 = (f32[4,256,128]{1,2,0:T(8,128)S(1)}, f32[4,256,128]{1,2,0:T(8,128)S(1)}, u32[]{:S(2)}, u32[]{:S(2)}) collective-permute-start(f32[4,256,128]{1,2,0:T(8,128)S(1)} %add.104), channel_id=1, source_target_pairs={{0,2},{1,3},{2,0},{3,1},{4,6},{5,7},{6,4},{7,5},{8,10},{9,11},{10,... | collective-permute-start | bytes 1572872 | tf_op jit(solution)/shard_map/ppermute | solution.py:48
  108.8 113.4 %all-reduce.4.cloned.1.call-start = ((), (), s32[]{:S(2)}) async-start(), calls=%async_computation.2 | async-start | bytes 1048576 | tf_op jit(solution)/shard_map/psum | solution.py:74
  111.7 79.0 %copy-start.4 = (f32[2,512,128]{2,1,0:T(8,128)S(1)}, f32[2,512,128]{2,1,0:T(8,128)}, u32[]{:S(2)}) copy-start(f32[2,512,128]{2,1,0:T(8,128)} %param.13) | copy-start | bytes 1572868
  190.7 107.5 %all-gather.10.cloned.1.call-start = ((), (), s32[]{:S(2)}) async-start(), calls=%async_computation.3 | async-start | bytes 4718592 | tf_op jit(solution)/shard_map/all_gather | solution.py:40
  224.1 169.8 %all-gather.12.cloned.1.call-start = ((), (), s32[]{:S(2)}) async-start(), calls=%async_computation.4 | async-start | bytes 4718592 | tf_op jit(solution)/shard_map/all_gather | solution.py:40
  224.2 98.1 %copy-start.7 = (s32[2,64,32]{1,2,0:T(8,128)S(1)}, s32[2,64,32]{1,2,0:T(8,128)}, u32[]{:S(2)}) copy-start(s32[2,64,32]{1,2,0:T(8,128)} %param.23) | copy-start | bytes 49156
  224.2 98.2 %copy-start.8 = (s32[4,64,16]{1,2,0:T(8,128)S(1)}, s32[4,64,16]{1,2,0:T(8,128)}, u32[]{:S(2)}) copy-start(s32[4,64,16]{1,2,0:T(8,128)} %param.22) | copy-start | bytes 49156
  305.1 2.0 collective-permute-start.2
  307.2 14.0 %collective-permute-start.3 = (f32[2,512,128]{1,2,0:T(8,128)S(1)}, f32[2,512,128]{1,2,0:T(8,128)S(1)}, u32[]{:S(2)}, u32[]{:S(2)}) collective-permute-start(f32[2,512,128]{1,2,0:T(8,128)S(1)} %add.111), channel_id=1, source_target_pairs={{0,2},{1,3},{2,0},{3,1},{4,6},{5,7},{6,4},{7,5},{8,10},{9,11},{10,... | collective-permute-start | bytes 1572872 | tf_op jit(solution)/shard_map/ppermute | solution.py:48
  322.1 117.7 %all-reduce.6.cloned.1.call-start = ((), (), s32[]{:S(2)}) async-start(), calls=%async_computation.6 | async-start | bytes 2097152 | tf_op jit(solution)/shard_map/psum | solution.py:78
  322.8 5.9 %slice-start = ((s8[8388608]{0:T(1024)(128)(4,1)}), s8[4194304]{0:T(1024)(128)(4,1)S(1)}, s32[]{:S(2)}) async-start(s8[8388608]{0:T(1024)(128)(4,1)} %bitcast.59), calls=%async_computation.7 | async-start | bytes 8388608
  324.1 4.6 slice-start.1
  337.4 102.4 %copy-start.5 = (f32[1024,128]{1,0:T(8,128)S(1)}, f32[1024,128]{1,0:T(8,128)}, u32[]{:S(2)}) copy-start(f32[1024,128]{1,0:T(8,128)} %param.14) | copy-start | bytes 1572868
  405.2 111.4 %all-gather.14.cloned.1.call-start = ((), (), s32[]{:S(2)}) async-start(), calls=%async_computation.5 | async-start | bytes 4718592 | tf_op jit(solution)/shard_map/all_gather | solution.py:40
  441.9 88.9 %copy-start.2 = (f32[4,256,128]{1,2,0:T(8,128)S(1)}, f32[4,256,128]{1,2,0:T(8,128)}, u32[]{:S(2)}) copy-start(f32[4,256,128]{1,2,0:T(8,128)} %add.105) | copy-start | bytes 1572868
  441.9 89.8 %copy-start.3 = (f32[2,512,128]{1,2,0:T(8,128)S(1)}, f32[2,512,128]{1,2,0:T(8,128)}, u32[]{:S(2)}) copy-start(f32[2,512,128]{1,2,0:T(8,128)} %add.112) | copy-start | bytes 1572868
  516.5 29.3 %copy-start.1 = (f32[4,256,512]{2,1,0:T(8,128)S(1)}, f32[4,256,512]{2,1,0:T(8,128)}, u32[]{:S(2)}) copy-start(f32[4,256,512]{2,1,0:T(8,128)} %param.15) | copy-start | bytes 6291460
  526.4 2.0 collective-permute-start.4
  529.3 14.3 %collective-permute-start.5 = (f32[1,1024,128]{1,2,0:T(8,128)}, f32[1,1024,128]{1,2,0:T(8,128)}, u32[]{:S(2)}, u32[]{:S(2)}) collective-permute-start(f32[1,1024,128]{1,2,0:T(8,128)} %add.118), channel_id=1, source_target_pairs={{0,2},{1,3},{2,0},{3,1},{4,6},{5,7},{6,4},{7,5},{8,10},{9,11},{10,... | collective-permute-start | bytes 1572872 | tf_op jit(solution)/shard_map/ppermute | solution.py:48
Sparse Core Ops, SparseCore 0:
  10.6 77.7 all-gather.5
  108.9 73.1 all-gather.7
  190.8 31.3 all-reduce.3
  224.8 73.3 all-gather.9
  322.2 71.6 all-gather.11
  405.3 34.4 all-reduce.5
  442.7 73.8 all-gather.13
